TPU v7x, 512 devices: a whole 4x4x16 slice. The times are simulated.
512 devices in a mesh: req: 64 (over z, y), hid: 8 (over x, core).
Axes of the slice: x: 4, y: 4, z: 16, core: 2. Of those that a mesh axis runs over, the one named last changes fastest.
Arguments:
- resid: bfloat16 [8192, 1024], P('req'), may hold values from -6 to 6
- attn_gain: float32 [1024], replicated, may hold values from 0.25 to 1.75
- w_query: bfloat16 [1024, 1024], P(None, 'hid'), may hold values from -4 to 4
- w_key: bfloat16 [1024, 1024], P(None, 'hid'), may hold values from -1 to 1
- w_value: bfloat16 [1024, 1024], P(None, 'hid'), may hold values from -0.1875 to 0.1875
- w_attn_out: bfloat16 [1024, 1024], P('hid'), may hold values from -0.1875 to 0.1875
- cache: bfloat16 [2048, 2, 16, 1024], P('req', None, None, 'hid'), may hold values from -48 to 48
- cache_lens: int32 [2048], P('req'), may hold values from 1 to 16
- seg_ids: int32 [64, 96], P('req'), may hold values from 0 to 3, never falling along the last dimension, each value on 1 to 48 neighbouring positions
- ffn_gain: float32 [1024], replicated, may hold values from 0.25 to 1.75
- router: bfloat16 [1024, 16], replicated, may hold values from -0.078125 to 0.078125
- routes: int32 [8192, 2], P('req'), may hold values from 0 to 15, all different within a row; in each aligned block of 16 rows (0 to 15, 16 to 31, ...) at most 3 rows name the same one
- w_in: bfloat16 [2, 1024, 45056], P(None, None, ('req', 'hid')), may hold values from -0.1875 to 0.1875
- w_out: bfloat16 [45056, 1024], P('req'), may hold values from -0.109375 to 0.109375
Outputs:
- layer_out: bfloat16 [8192, 1024], P(('req', 'hid'))
Inputs may be any that keep to these rules, and one draw needn't show every extreme that they name: `routes`: in every aligned block of 16 rows no expert is named more than 3 times, so no assignment is dropped.
All inputs are finite; a program needn't handle non-finite values.
Results may differ from a plain program's by a relative error of at most 0.012.
The roundings to bfloat16 on the way count: a program that leaves them out, or rounds other values in their place, can miss the bound.
Values may be sent and summed in bfloat16 or wider, within the bound.
No kernel may reach another device: no remote copies, remote signals or barrier semaphores. Data moves between devices by JAX's collectives and lax.ppermute only.
A program may use at most 64 MiB of HBM per device.

v0:
```python
import jax
import jax.numpy as jnp
from jax import lax
from jax.sharding import PartitionSpec as P

HDIM = 64


EPS = 1e-06


def rms_scale(values, gain):
    values = values.astype(jnp.float32)
    inverse = lax.rsqrt(jnp.mean(values * values, axis=-1, keepdims=True) + EPS)
    return (values * inverse * gain).astype(jnp.bfloat16)


def softmax_bf16(scores, allowed):
    scores = jnp.where(allowed, scores, -jnp.inf)
    highest = jnp.max(scores, axis=-1, keepdims=True)
    weights = jnp.exp(scores - highest)
    return (weights / jnp.sum(weights, axis=-1, keepdims=True)).astype(jnp.bfloat16)


def attend(normed, w_query, w_key, w_value, segments, cached, lengths):
    heads = w_query.shape[1] // HDIM
    scale = HDIM ** (-0.5)
    total = normed.shape[0]
    packed = segments.shape[0]
    decoded = total - packed
    slots = cached.shape[2]
    query = (
        jnp.dot(normed, w_query, preferred_element_type=jnp.float32)
        .astype(jnp.bfloat16)
        .reshape(total, heads, HDIM)
    )
    keys = (
        jnp.dot(normed, w_key, preferred_element_type=jnp.float32)
        .astype(jnp.bfloat16)
        .reshape(total, heads, HDIM)
    )
    values = (
        jnp.dot(normed, w_value, preferred_element_type=jnp.float32)
        .astype(jnp.bfloat16)
        .reshape(total, heads, HDIM)
    )
    positions = jnp.arange(packed)
    allowed = (positions[None, :] <= positions[:, None]) & (segments[None, :] == segments[:, None])
    scores = (
        jnp.einsum(
            "qhd,khd->hqk", query[:packed], keys[:packed], preferred_element_type=jnp.float32
        )
        * scale
    )
    weights = softmax_bf16(scores, allowed[None])
    prompt_ctx = jnp.einsum(
        "hqk,khd->qhd", weights, values[:packed], preferred_element_type=jnp.float32
    )
    stored = cached.reshape(decoded, 2, slots, heads, HDIM)
    cached_scores = (
        jnp.einsum(
            "uhd,uchd->uhc", query[packed:], stored[:, 0], preferred_element_type=jnp.float32
        )
        * scale
    )
    own_scores = (
        jnp.sum(
            query[packed:].astype(jnp.float32) * keys[packed:].astype(jnp.float32),
            axis=-1,
            keepdims=True,
        )
        * scale
    )
    valid = jnp.arange(slots)[None, None, :] < lengths[:, None, None]
    allowed_all = jnp.concatenate(
        [jnp.broadcast_to(valid, cached_scores.shape), jnp.ones(own_scores.shape, dtype=bool)],
        axis=-1,
    )
    joined = jnp.concatenate([cached_scores, own_scores], axis=-1)
    weights_dec = softmax_bf16(joined, allowed_all)
    decode_ctx = jnp.einsum(
        "uhc,uchd->uhd", weights_dec[..., :slots], stored[:, 1], preferred_element_type=jnp.float32
    )
    decode_ctx = decode_ctx + weights_dec[..., slots:].astype(jnp.float32) * values[packed:].astype(
        jnp.float32
    )
    context = jnp.concatenate([prompt_ctx, decode_ctx], axis=0)
    return context.reshape(total, heads * HDIM).astype(jnp.bfloat16)


def route_block(chosen, gate_logits, capacity):
    count = chosen.shape[0]
    experts = gate_logits.shape[1]
    flat = chosen.reshape(count * 2)
    onehot = (flat[:, None] == jnp.arange(experts, dtype=jnp.int32)[None, :]).astype(jnp.int32)
    earlier = jnp.cumsum(onehot, axis=0) - onehot
    slot = jnp.sum(earlier * onehot, axis=1)
    target = flat * capacity + slot
    placed = (target[:, None] == jnp.arange(experts * capacity, dtype=jnp.int32)[None, :]).astype(
        jnp.float32
    )
    placed = placed.reshape(count, 2, experts * capacity)
    picked_logits = jnp.sum(
        onehot.reshape(count, 2, experts).astype(jnp.float32) * gate_logits[:, None, :], axis=-1
    )
    gates = jax.nn.sigmoid(picked_logits)
    dispatch = jnp.sum(placed, axis=1).astype(jnp.bfloat16)
    combine_w = jnp.sum(placed * gates[:, :, None], axis=1)
    return (dispatch, combine_w)


def hidden_units(tokens_in, w_in):
    gate_val = jnp.dot(tokens_in, w_in[0], preferred_element_type=jnp.float32)
    up_val = jnp.dot(tokens_in, w_in[1], preferred_element_type=jnp.float32)
    return (jax.nn.gelu(gate_val, approximate=True) * up_val).astype(jnp.bfloat16)


def body(
    resid,
    attn_gain,
    w_query,
    w_key,
    w_value,
    w_attn_out,
    cache,
    cache_lens,
    seg_ids,
    ffn_gain,
    router,
    routes,
    w_in,
    w_out,
):
    req_count = lax.axis_size("req")
    hid_count = lax.axis_size("hid")
    hid_index = lax.axis_index("hid")
    experts = router.shape[1]
    replicas = req_count // experts
    group_rows = resid.shape[0]
    block_rows = group_rows // hid_count
    capacity = max(2, (5 * block_rows + 31) // 32)
    width = resid.shape[1]
    row_start = hid_index * block_rows
    normed = rms_scale(resid, attn_gain)
    context = attend(normed, w_query, w_key, w_value, seg_ids[0], cache, cache_lens)
    partial_mix = jnp.dot(context, w_attn_out, preferred_element_type=jnp.float32)
    mixed = lax.psum(partial_mix, "hid")
    after = resid.astype(jnp.float32) + mixed
    full_ffn = rms_scale(after, ffn_gain)
    own_after = lax.dynamic_slice_in_dim(after, row_start, block_rows, 0)
    logits = jnp.dot(full_ffn, router, preferred_element_type=jnp.float32)
    all_routes = routes.reshape(hid_count, block_rows, 2)
    all_logits = logits.reshape(hid_count, block_rows, experts)
    dispatch_all, combine_all = jax.vmap(
        lambda chosen, gate_logits: route_block(chosen, gate_logits, capacity)
    )(all_routes, all_logits)
    combine_w = lax.dynamic_index_in_dim(combine_all, hid_index, 0, keepdims=False)
    all_tokens = full_ffn.reshape(hid_count, block_rows, width)
    outgoing = jnp.einsum(
        "nbs,nbd->nsd", dispatch_all, all_tokens, preferred_element_type=jnp.float32
    ).astype(jnp.bfloat16)
    outgoing = jnp.broadcast_to(
        outgoing.reshape(hid_count, experts, 1, capacity, width),
        (hid_count, experts, replicas, capacity, width),
    )
    outgoing = outgoing.reshape(hid_count, req_count, capacity, width)
    received = lax.all_to_all(outgoing, "req", split_axis=1, concat_axis=1, tiled=True)
    hidden = hidden_units(received.reshape(hid_count * req_count * capacity, width), w_in)
    stacked = hidden.reshape(hid_count, req_count * capacity, hidden.shape[1])
    projected = jnp.dot(
        lax.all_to_all(stacked, "hid", split_axis=0, concat_axis=2, tiled=True)[0],
        w_out,
        preferred_element_type=jnp.float32,
    ).astype(jnp.bfloat16)[None]
    returned = lax.all_to_all(
        projected.reshape(req_count * capacity, width),
        "req",
        split_axis=0,
        concat_axis=0,
        tiled=True,
    )
    summed = jnp.sum(
        returned.astype(jnp.float32).reshape(experts, replicas, capacity, width), axis=1
    )
    ffn_total = jnp.dot(
        combine_w,
        summed.reshape(experts * capacity, width),
        precision=lax.Precision.HIGHEST,
        preferred_element_type=jnp.float32,
    )
    return (own_after + ffn_total).astype(jnp.bfloat16)


def solution(mesh):
    in_specs = (
        P("req", None),
        P(),
        P(None, "hid"),
        P(None, "hid"),
        P(None, "hid"),
        P("hid", None),
        P("req", None, None, "hid"),
        P("req"),
        P("req", None),
        P(),
        P(),
        P("req", None),
        P(None, None, ("req", "hid")),
        P("req", None),
    )
    out_specs = P(("req", "hid"), None)
    return jax.shard_map(body, mesh=mesh, in_specs=in_specs, out_specs=out_specs, check_vma=False)
```

profile of v0, /device:TPU:6, one launch (start us, length us, event | category | flops | bytes accessed | tf_op | source)
XLA Modules:
  0.0 337.0 jit_solution(14188825207988231362)
XLA Ops:
  6.5 0.0 copy-start
  6.6 0.0 all-reduce.3.cloned.1.call-start
  6.6 1.2 fusion.15
  7.8 1.3 convolution_convert_fusion.4
  9.2 0.0 copy-start.3
  9.2 0.1 slice.58
  9.3 0.1 reshape.189
  9.4 1.3 convolution_convert_fusion.3
  10.7 0.1 reshape.180
  10.8 0.1 multiply_reduce_fusion.3
  10.9 0.1 copy.114
  11.0 1.2 reshape.174
  12.2 0.2 slice_bitcast_fusion.1
  12.4 0.2 fusion.18
  12.7 0.1 copy.103
  12.8 0.0 copy-done.9
  12.8 0.0 copy-start.6
  13.0 0.1 copy.83
  13.1 0.1 copy.84
  13.2 0.1 fusion.27
  13.3 0.2 fusion.5
  13.5 0.3 fusion.44
  13.8 0.0 copy-start.5
  13.8 0.3 convolution_convert_fusion.5
  14.2 0.2 copy.113
  14.4 0.7 multiply_reduce_fusion
  15.1 0.1 copy.109
  15.2 0.1 copy.110
  15.3 0.1 copy.82
  15.4 0.2 fusion.7
  15.6 0.1 pad_maximum_fusion
  15.7 1.1 fusion.46
  16.8 0.0 all-reduce.3.cloned.1.call-update
  16.8 0.1 copy.88
  16.9 0.1 eq.58
  17.0 0.1 copy.89
  17.1 0.7 fusion.45
  17.8 0.1 reshape_reshape.4
  17.9 0.1 copy.90
  18.0 77.1 %all-reduce.3.cloned.1.call-done = f32[128,1024]{1,0:T(8,128)} async-done(((f32[128,1024]{1,0:T(8,128)}), f32[128,1024]{1,0:T(8,128)}) %all-reduce.3.cloned.1.call-update) | async-done | bytes 524304 | tf_op jit(solution)/shard_map/psum | solution.py:147
  95.1 1.2 multiply_reduce_fusion.1
  96.3 0.1 multiply_convert_fusion
  96.5 0.2 fusion.47
  96.7 0.2 multiply_reduce_fusion.2
  96.9 0.1 select_reduce_fusion
  97.1 0.4 convolution_convert_fusion
  97.5 0.4 copy.96
  97.9 0.4 broadcast_in_dim.27
  98.3 161.6 %all_to_all.29 = bf16[8,64,3,1024]{3,0,2,1:T(8,128)(2,1)S(1)} all-to-all(bf16[8,64,3,1024]{3,0,2,1:T(8,128)(2,1)S(1)} %bitcast.73), channel_id=1, replica_groups=mesh['req'=64,'hid'=8] {'req'}, dimensions={1} | all-to-all | bytes 6291456 | tf_op jit(solution)/shard_map/all_to_all | solution.py:167
  259.9 4.6 %copy.97 = bf16[8,64,3,1024]{3,2,1,0:T(4,128)(2,1)} copy(bf16[8,64,3,1024]{3,0,2,1:T(8,128)(2,1)S(1)} %all_to_all.29) | data formatting | bytes 6291456 | tf_op jit(solution)/shard_map/all_to_all | solution.py:167
  264.6 8.9 %reshape.177 = bf16[1536,1024]{1,0:T(8,128)(2,1)} reshape(bf16[8,64,3,1024]{3,2,1,0:T(4,128)(2,1)} %copy.97) | data formatting | bytes 6291456 | tf_op jit(solution)/shard_map/reshape | solution.py:168
  273.4 3.1 fusion.21
  276.5 0.0 copy-done.1
  276.6 1.1 fusion.1
  277.7 0.3 reshape.178
  278.0 0.1 copy.98
  278.0 10.8 %all_to_all.30 = bf16[8,192,88]{1,2,0:T(8,128)(2,1)S(1)} all-to-all(bf16[8,192,88]{1,2,0:T(8,128)(2,1)S(1)} %copy.98), channel_id=1, replica_groups=mesh['req'=64,'hid'=8] {'hid'}, dimensions={0} | all-to-all | bytes 540672 | tf_op jit(solution)/shard_map/all_to_all | solution.py:171
  288.9 0.5 convolution_convert_fusion.1
  289.4 1.0 all_to_all.24
  290.4 5.8 %all-to-all-start.2 = ((bf16[64,3,1024]{2,1,0:T(4,128)(2,1)}), bf16[64,3,1024]{2,1,0:T(4,128)(2,1)S(1)}, u32[]{:S(2)}, u32[]{:S(2)}) async-start(bf16[64,3,1024]{2,1,0:T(4,128)(2,1)} %all_to_all.24), calls=%async_computation.2 | async-start | bytes 1048576 | tf_op jit(solution)/shard_map/all_to_all | solution.py:175
  296.3 32.7 %all-to-all-done.2 = bf16[64,3,1024]{2,1,0:T(4,128)(2,1)S(1)} async-done(((bf16[64,3,1024]{2,1,0:T(4,128)(2,1)}), bf16[64,3,1024]{2,1,0:T(4,128)(2,1)S(1)}, u32[]{:S(2)}, u32[]{:S(2)}) %all-to-all-start.2) | async-done | bytes 393248 | tf_op jit(solution)/shard_map/all_to_all | solution.py:175
  328.9 0.2 convert_reduce_fusion
  329.2 0.1 reshape.179
  329.3 0.8 fusion.6
  (41 shorter events, 0.3 us)
Async XLA Ops:
  6.5 282.3 %copy-start = (bf16[704,1024]{1,0:T(8,128)(2,1)S(1)}, bf16[704,1024]{1,0:T(8,128)(2,1)}, u32[]{:S(2)}) copy-start(bf16[704,1024]{1,0:T(8,128)(2,1)} %param.27) | copy-start | bytes 4325380
  6.5 7.3 %copy-start.2 = (bf16[128,1024]{1,0:T(8,128)(2,1)S(1)}, bf16[128,1024]{1,0:T(8,128)(2,1)}, u32[]{:S(2)}) copy-start(bf16[128,1024]{1,0:T(8,128)(2,1)} %param.14) | copy-start | bytes 786436
  6.5 7.3 %copy-start.11 = (f32[1024]{0:T(1024)S(1)}, f32[1024]{0:T(1024)}, u32[]{:S(2)}) copy-start(f32[1024]{0:T(1024)} %param.15) | copy-start | bytes 12292
  6.5 6.2 %copy-start.9 = (s32[32]{0:T(128)S(1)}, s32[32]{0:T(128)}, u32[]{:S(2)}) copy-start(s32[32]{0:T(128)} %param.21) | copy-start | bytes 388
  6.5 6.7 %copy-start.8 = (s32[1,96]{1,0:T(1,128)S(1)}, s32[1,96]{1,0:T(1,128)}, u32[]{:S(2)}) copy-start(s32[1,96]{1,0:T(1,128)} %param.22) | copy-start | bytes 1156
  6.5 7.3 %copy-start.10 = (bf16[1024,128]{1,0:T(8,128)(2,1)S(1)}, bf16[1024,128]{1,0:T(8,128)(2,1)}, u32[]{:S(2)}) copy-start(bf16[1024,128]{1,0:T(8,128)(2,1)} %param.18) | copy-start | bytes 786436
  6.6 88.6 %all-reduce.3.cloned.1.call-start = ((), (), s32[]{:S(2)}) async-start(), calls=%async_computation.3 | async-start | bytes 1048576 | tf_op jit(solution)/shard_map/psum | solution.py:147
  9.2 6.5 %copy-start.3 = (bf16[128,1024]{1,0:T(8,128)(2,1)S(1)}, bf16[128,1024]{1,0:T(8,128)(2,1)}, u32[]{:S(2)}) copy-start(bf16[128,1024]{1,0:T(8,128)(2,1)} %param.19) | copy-start | bytes 786436
  11.0 5.8 %copy-start.7 = (s32[128,2]{0,1:T(2,128)S(1)}, s32[128,2]{0,1:T(2,128)}, u32[]{:S(2)}) copy-start(s32[128,2]{0,1:T(2,128)} %param.25) | copy-start | bytes 3076
  12.8 83.5 %copy-start.6 = (f32[1024]{0:T(1024)S(1)}, f32[1024]{0:T(1024)}, u32[]{:S(2)}) copy-start(f32[1024]{0:T(1024)} %param.23) | copy-start | bytes 12292
  13.8 82.6 %copy-start.5 = (bf16[1024,16]{0,1:T(8,128)(2,1)S(1)}, bf16[1024,16]{0,1:T(8,128)(2,1)}, u32[]{:S(2)}) copy-start(bf16[1024,16]{0,1:T(8,128)(2,1)} %param.24) | copy-start | bytes 98308
  264.6 8.9 %copy-start.4 = (bf16[2,1024,88]{1,2,0:T(8,128)(2,1)S(1)}, bf16[2,1024,88]{1,2,0:T(8,128)(2,1)}, u32[]{:S(2)}) copy-start(bf16[2,1024,88]{1,2,0:T(8,128)(2,1)} %param.26) | copy-start | bytes 1081348
  273.4 3.1 copy-start.1
  290.4 38.5 %all-to-all-start.2 = ((bf16[64,3,1024]{2,1,0:T(4,128)(2,1)}), bf16[64,3,1024]{2,1,0:T(4,128)(2,1)S(1)}, u32[]{:S(2)}, u32[]{:S(2)}) async-start(bf16[64,3,1024]{2,1,0:T(4,128)(2,1)} %all_to_all.24), calls=%async_computation.2 | async-start | bytes 1048576 | tf_op jit(solution)/shard_map/all_to_all | solution.py:175
Sparse Core Ops, SparseCore 0:
  16.9 78.1 all-reduce.2
where the time goes:
time: 339 us; the launch traced here: 337 us
  blocking collectives  172 us (51%)
  waiting for transfers between devices  110 us (32%)
  local copies, waits for them, and re-layouts  18.9 us (6%)
  between operations  13.9 us (4%)
  matrix products  11.1 us (3%)
  starting transfers between devices  5.87 us (2%)
  other arithmetic  5.03 us (1%)
    all_to_all x1, blocking collectives, body(): lax.all_to_all(outgoing, 'req', split_axis=1, concat_axis=1, tiled=True)  162 us
    psum x1, waiting for transfers between devices, body(): mixed = lax.psum(partial_mix, 'hid')  77.1 us
    all_to_all x1, waiting for transfers between devices, body(): lax.all_to_all(projected.reshape(req_count * capacity, width), 'req', spl...  32.7 us
    all_to_all x1, blocking collectives, body(): lax.all_to_all(stacked, 'hid', split_axis=0, concat_axis=2, tiled=True)[0]  10.8 us
    reshape x1, local copies, waits for them, and re-layouts, body(): received.reshape(hid_count * req_count * capacity, width)  8.86 us
  transfers between devices with their start and end apart: 2, of which 2 were waited for; matrix products, arithmetic and copies ran while one was open for 0% of the time, Pallas kernels for 0%

commit v1 on v0

v1 whole, which is shorter than its diff:
```python
import jax
import jax.numpy as jnp
from jax import lax
from jax.experimental import pallas as pl
from jax.experimental.pallas import tpu as pltpu
from jax.sharding import Mesh
from jax.sharding import PartitionSpec as P

HDIM = 64
EPS = 1e-06
BF = jnp.bfloat16
F32 = jnp.float32
LANES = 128


def dot(a, b):
    return jnp.dot(a, b, preferred_element_type=F32)


def dot_nt(a, b):
    return lax.dot_general(a, b, (((1,), (1,)), ((), ())), preferred_element_type=F32)


def dot_tn(a, b):
    return lax.dot_general(a, b, (((0,), (0,)), ((), ())), preferred_element_type=F32)


def iota(shape, dim):
    return lax.broadcasted_iota(jnp.int32, shape, dim)


def to_column(row, size):
    diagonal = iota((size, size), 0) == iota((size, size), 1)
    return jnp.sum(jnp.where(diagonal, jnp.broadcast_to(row, (size, size)), 0), axis=1, keepdims=True)


def attention_kernel(
    resid_ref, gain_ref, wq_ref, wk_ref, wv_ref, wo_ref, cache_ref, lens_ref, seg_ref, out_ref, seg_row
):
    total = resid_ref.shape[0]
    packed = seg_ref.shape[1]
    decoded, _, slots, width = cache_ref.shape
    heads = width // HDIM
    scale = HDIM ** (-0.5)
    x = resid_ref[...].astype(F32)
    inverse = lax.rsqrt(jnp.mean(x * x, axis=-1, keepdims=True) + EPS)
    normed = (x * inverse * gain_ref[...]).astype(BF)
    query = dot(normed, wq_ref[...]).astype(BF)
    keys = dot(normed, wk_ref[...]).astype(BF)
    values = dot(normed, wv_ref[...]).astype(BF)

    seg_row[...] = iota((1, total), 1) + (1 << 20)
    seg_row[:, :packed] = seg_ref[...]
    segments = seg_row[...]
    allowed = (iota((total, total), 1) <= iota((total, total), 0)) & (to_column(segments, total) == segments)
    lengths = to_column(lens_ref[...], decoded)
    slot_at = iota((decoded, decoded * slots), 1)
    own_cache = (slot_at // slots == iota((decoded, decoded * slots), 0)) & (slot_at % slots < lengths)

    cached_keys = cache_ref[:, 0].reshape(decoded * slots, width)
    cached_values = cache_ref[:, 1].reshape(decoded * slots, width)
    lane_head = iota((total, width), 1) // HDIM
    context = jnp.zeros((total, width), F32)
    for head in range(heads):
        mine = lane_head == head
        head_query = jnp.where(mine, query, jnp.zeros_like(query))
        scores = jnp.where(allowed, dot_nt(head_query, keys) * scale, -jnp.inf)
        highest = jnp.max(scores, axis=-1, keepdims=True)
        cached = jnp.where(own_cache, dot_nt(head_query[packed:], cached_keys) * scale, -jnp.inf)
        top_dec = jnp.maximum(highest[packed:], jnp.max(cached, axis=-1, keepdims=True))
        highest = jnp.concatenate([highest[:packed], top_dec], axis=0)
        weights = jnp.exp(scores - highest)
        weights_cache = jnp.exp(cached - top_dec)
        norm = jnp.sum(weights, axis=-1, keepdims=True)
        norm_dec = norm[packed:] + jnp.sum(weights_cache, axis=-1, keepdims=True)
        norm = jnp.concatenate([norm[:packed], norm_dec], axis=0)
        part = dot((weights / norm).astype(BF), values)
        part_cache = dot((weights_cache / norm_dec).astype(BF), cached_values)
        part = jnp.concatenate([part[:packed], part[packed:] + part_cache], axis=0)
        context = jnp.where(mine, part, context)
    out_ref[...] = dot(context.astype(BF), wo_ref[...]).astype(out_ref.dtype)


def own_routes(routes_ref, which, index, block):
    lane = iota((1, LANES), 1)
    row = pltpu.roll(routes_ref[pl.ds(which, 1), :], (LANES - index * block) % LANES, 1)
    size = block
    while size < LANES:
        row = jnp.where(lane < size, row, pltpu.roll(row, size, 1))
        size *= 2
    return row


def placement(row, columns, block, capacity, chunks):
    token = iota((block, LANES), 1) % block
    before = iota((block, LANES), 0) < token
    slot = jnp.zeros((1, LANES), jnp.int32)
    for column in columns:
        slot = slot + jnp.sum(((column == row) & before).astype(jnp.int32), axis=0, keepdims=True)
    target = row * capacity + slot
    return target


def slot_rows(rows, capacity, chunks):
    at = iota((rows, LANES), 0)
    expert = at // (chunks * capacity)
    rest = at - expert * (chunks * capacity)
    chunk = rest // capacity
    return expert * capacity + rest - chunk * capacity, chunk


def route_columns(rows, block):
    size = (block, LANES)
    diagonal = iota(size, 0) == iota(size, 1)
    return [
        jnp.sum(jnp.where(diagonal, jnp.broadcast_to(row, size), 0), axis=1, keepdims=True) for row in rows
    ]


def dispatch_kernel(
    index_ref, parts_ref, resid_ref, gain_ref, router_ref, routes_ref, out_ref, after_ref, gates_ref, target_ref
):
    sources, block, width = parts_ref.shape
    experts = router_ref.shape[0]
    chunks = width // LANES
    capacity = out_ref.shape[0] // (experts * chunks)
    index = index_ref[0]
    start = pl.multiple_of(index * block, block)
    mixed = parts_ref[0].astype(F32)
    for source in range(1, sources):
        mixed = mixed + parts_ref[source].astype(F32)
    after = resid_ref[pl.ds(start, block), :].astype(F32) + mixed
    after_ref[...] = after
    inverse = lax.rsqrt(jnp.mean(after * after, axis=-1, keepdims=True) + EPS)
    ffn_in = (after * inverse * gain_ref[...]).astype(BF)
    rows = [own_routes(routes_ref, which, index, block) for which in range(2)]
    columns = route_columns(rows, block)
    targets = [placement(row, columns, block, capacity, chunks) for row in rows]
    wanted, chunk = slot_rows(out_ref.shape[0], capacity, chunks)
    same = chunk == iota(chunk.shape, 1) // block
    chosen = same & ((wanted == targets[0]) | (wanted == targets[1]))
    stacked = jnp.concatenate([ffn_in[:, at * LANES : (at + 1) * LANES] for at in range(chunks)], axis=0)
    out_ref[...] = dot(jnp.where(chosen, 1.0, 0.0).astype(BF), stacked).astype(BF)
    logits = dot_nt(ffn_in, router_ref[...])
    expert_at = iota((block, experts), 1)
    for which in range(2):
        picked = jnp.sum(jnp.where(expert_at == columns[which], logits, 0.0), axis=1, keepdims=True)
        gates_ref[which] = jnp.broadcast_to(jax.nn.sigmoid(picked), (block, LANES))
        target_ref[pl.ds(which, 1), :] = targets[which]


def ffn_kernel(tokens_ref, gate_ref, up_ref, down_ref, out_ref, rows_ref):
    groups, chunk_rows, _ = tokens_ref.shape
    width = rows_ref.shape[1]
    chunks = width // LANES
    each = chunk_rows // chunks
    capacity = 3
    at = iota((chunk_rows, chunk_rows), 0)
    chunk = at // each
    rest = at - chunk * each
    source = rest // capacity
    wanted = source * (chunks * capacity) + chunk * capacity + rest - source * capacity
    order = jnp.where(wanted == iota((chunk_rows, chunk_rows), 1), 1.0, 0.0).astype(BF)
    for group in range(groups):
        unpacked = dot(order, tokens_ref[group]).astype(BF)
        for at in range(chunks):
            rows_ref[group * each : (group + 1) * each, at * LANES : (at + 1) * LANES] = unpacked[
                at * each : (at + 1) * each
            ]
    rows = rows_ref[...]
    gate_val = dot_nt(rows, gate_ref[...])
    up_val = dot_nt(rows, up_ref[...])
    hidden = (jax.nn.gelu(gate_val, approximate=True) * up_val).astype(BF)
    parts = dot(hidden, down_ref[...]).astype(BF)
    for group in range(groups):
        mine = parts[group * each : (group + 1) * each]
        stacked = jnp.concatenate([mine[:, at * LANES : (at + 1) * LANES] for at in range(chunks)], axis=0)
        out_ref[group] = dot_tn(order, stacked).astype(BF)


def combine_kernel(experts_ref, after_ref, gates_ref, target_ref, out_ref):
    rows = experts_ref.shape[0]
    block, width = after_ref.shape
    chunks = width // LANES
    capacity = 3
    wanted, chunk = slot_rows(rows, capacity, chunks)
    same = chunk == iota(chunk.shape, 1) // block
    outputs = experts_ref[...]
    picked = []
    for which in range(2):
        chosen = same & (wanted == target_ref[pl.ds(which, 1), :])
        picked.append(dot_tn(jnp.where(chosen, 1.0, 0.0).astype(BF), outputs))
    for at in range(chunks):
        lanes = slice(at * LANES, (at + 1) * LANES)
        mine = slice(at * block, (at + 1) * block)
        total = gates_ref[0] * picked[0][mine] + gates_ref[1] * picked[1][mine]
        out_ref[:, lanes] = (after_ref[:, lanes] + total).astype(BF)


VMEM = pl.BlockSpec(memory_space=pltpu.VMEM)
SMEM = pl.BlockSpec(memory_space=pltpu.SMEM)
PARAMS = pltpu.CompilerParams(vmem_limit_bytes=40 * 1024 * 1024)


def body(
    resid, attn_gain, w_query, w_key, w_value, w_attn_out, cache, cache_lens, seg_ids, ffn_gain, router, routes, w_in, w_out
):
    hid = ("x", "c")
    hid_count = lax.axis_size(hid)
    hid_index = lax.axis_index(hid).astype(jnp.int32).reshape(1)
    group_rows, width = resid.shape
    experts = router.shape[1]
    block = group_rows // hid_count
    capacity = 3
    chunks = width // LANES
    slot_count = experts * chunks * capacity
    split = lax.axis_size("y")
    w_cols = jnp.transpose(w_in, (0, 2, 1))
    w_gate = lax.all_gather(w_cols[0], hid, axis=0, tiled=True)
    w_up = lax.all_gather(w_cols[1], hid, axis=0, tiled=True)

    partial_mix = pl.pallas_call(
        attention_kernel,
        out_shape=jax.ShapeDtypeStruct((group_rows, width), BF),
        in_specs=[VMEM] * 9,
        out_specs=VMEM,
        scratch_shapes=[pltpu.VMEM((1, group_rows), jnp.int32)],
        compiler_params=PARAMS,
        name="attention",
    )(
        resid,
        attn_gain.reshape(1, width),
        w_query,
        w_key,
        w_value,
        w_attn_out,
        cache,
        cache_lens.reshape(1, -1),
        seg_ids,
    )
    parts = lax.all_to_all(partial_mix.reshape(hid_count, block, width), hid, 0, 0, tiled=True)
    outgoing, after, gates, target = pl.pallas_call(
        dispatch_kernel,
        out_shape=(
            jax.ShapeDtypeStruct((slot_count, LANES), BF),
            jax.ShapeDtypeStruct((block, width), F32),
            jax.ShapeDtypeStruct((2, block, LANES), F32),
            jax.ShapeDtypeStruct((2, LANES), jnp.int32),
        ),
        in_specs=[SMEM] + [VMEM] * 5,
        out_specs=(VMEM,) * 4,
        compiler_params=PARAMS,
        name="dispatch",
    )(hid_index, parts, resid, ffn_gain.reshape(1, width), router.T, routes.T)
    arrived = lax.all_to_all(outgoing.reshape(experts, chunks * capacity, LANES), "z", 0, 0, tiled=True)
    tokens = lax.all_gather(arrived.reshape(slot_count, LANES), "y", axis=0)
    projected = pl.pallas_call(
        ffn_kernel,
        out_shape=jax.ShapeDtypeStruct((split, slot_count, LANES), BF),
        in_specs=[VMEM] * 4,
        out_specs=VMEM,
        scratch_shapes=[pltpu.VMEM((split * experts * capacity, width), BF)],
        compiler_params=PARAMS,
        name="ffn",
    )(tokens, w_gate, w_up, w_out)
    quarters = lax.all_to_all(projected, "y", 0, 0, tiled=True)
    summed = jnp.sum(quarters.astype(F32), axis=0).astype(BF)
    returned = lax.all_to_all(summed.reshape(experts, chunks * capacity, LANES), "z", 0, 0, tiled=True)
    return pl.pallas_call(
        combine_kernel,
        out_shape=jax.ShapeDtypeStruct((block, width), BF),
        in_specs=[VMEM] * 4,
        out_specs=VMEM,
        compiler_params=PARAMS,
        name="combine",
    )(returned.reshape(slot_count, LANES), after, gates, target)


def solution(mesh):
    fine = Mesh(mesh.devices.reshape(16, 4, 4, 2), ("z", "y", "x", "c"))
    req = ("z", "y")
    hid = ("x", "c")
    in_specs = (
        P(req, None),
        P(),
        P(None, hid),
        P(None, hid),
        P(None, hid),
        P(hid, None),
        P(req, None, None, hid),
        P(req),
        P(req, None),
        P(),
        P(),
        P(req, None),
        P(None, None, req + hid),
        P(req, None),
    )
    out_specs = P(req + hid, None)
    return jax.shard_map(body, mesh=fine, in_specs=in_specs, out_specs=out_specs, check_vma=False)
```

time: 339 us -> 131 us (0.39)
  blocking collectives: 172 us -> 74.9 us
  waiting for transfers between devices: 110 us -> 13 us
  matrix products: 11.1 us -> 0 us
  local copies, waits for them, and re-layouts: 18.9 us -> 12.2 us
  Pallas kernels: 0 us -> 6.46 us
  other arithmetic: 5.03 us -> 0.06 us
    all_to_all x2 -> x3, blocking collectives: 172 us -> 61.5 us  [the longest x1 25.3 us: body(): lax.all_to_all(summed.reshape(experts, chunks * capacity, LANES), 'z', 0,...]
    psum x1 -> x0, waiting for transfers between devices: 77.1 us -> none  [body(): mixed = lax.psum(partial_mix, 'hid')]
    all_to_all x1, waiting for transfers between devices: 32.7 us -> 5.55 us  [body(): lax.all_to_all(partial_mix.reshape(hid_count, block, width), hid, 0, 0, t...]
    all_gather x0 -> x1, blocking collectives: none -> 13.4 us  [body(): tokens = lax.all_gather(arrived.reshape(slot_count, LANES), 'y', axis=0)]
    dot_general x12 -> x0, matrix products: 10.6 us -> none  [the longest x1 3.12 us: hidden_units(): gate_val = jnp.dot(tokens_in, w_in[0], preferred_element_type=jnp.float32)]
    reshape x5 -> x0, local copies, waits for them, and re-layouts: 10.5 us -> none  [the longest x1 8.86 us: body(): received.reshape(hid_count * req_count * capacity, width)]
    unnamed x27 -> x32, local copies, waits for them, and re-layouts: 0.44 us -> 10.4 us
    all_gather x0 -> x2, waiting for transfers between devices: none -> 6.75 us  [the longest x1 6.75 us: body(): w_gate = lax.all_gather(w_cols[0], hid, axis=0, tiled=True)]
  transfers between devices with their start and end apart: 2 -> 3, of which waited for: 2 -> 2; matrix products, arithmetic and copies ran while one was open for 0% -> 0% of each run, Pallas kernels for 0% -> 2%
where the time goes in v1:
time: 131 us; the launch traced here: 129 us
  blocking collectives  74.9 us (57%)
  between operations  13.5 us (10%)
  waiting for transfers between devices  13 us (10%)
  local copies, waits for them, and re-layouts  12.2 us (9%)
  starting transfers between devices  9.25 us (7%)
  Pallas kernels  6.46 us (5%)
    all_to_all x1, blocking collectives, body(): lax.all_to_all(summed.reshape(experts, chunks * capacity, LANES), 'z', 0,...  25.3 us
    all_to_all x1, blocking collectives, body(): lax.all_to_all(outgoing.reshape(experts, chunks * capacity, LANES), 'z',...  23.7 us
    all_gather x1, blocking collectives, body(): tokens = lax.all_gather(arrived.reshape(slot_count, LANES), 'y', axis=0)  13.4 us
    all_to_all x1, blocking collectives, body(): quarters = lax.all_to_all(projected, 'y', 0, 0, tiled=True)  12.5 us
    unnamed x32, local copies, waits for them, and re-layouts  10.4 us
    all_to_all x1, starting transfers between devices, body(): lax.all_to_all(partial_mix.reshape(hid_count, block, width), hid, 0, 0, t...  9.2 us
    all_gather x1, waiting for transfers between devices, body(): w_gate = lax.all_gather(w_cols[0], hid, axis=0, tiled=True)  6.75 us
    all_to_all x1, waiting for transfers between devices, body(): lax.all_to_all(partial_mix.reshape(hid_count, block, width), hid, 0, 0, t...  5.55 us
  transfers between devices with their start and end apart: 3, of which 2 were waited for; matrix products, arithmetic and copies ran while one was open for 0% of the time, Pallas kernels for 2%

profile of v1, /device:TPU:6, one launch (start us, length us, event | category | flops | bytes accessed | tf_op | source)
XLA Modules:
  0.0 129.3 jit_solution(6974432654532348868)
XLA Ops:
  6.5 0.0 all-gather.7.cloned.1.call-start
  6.5 1.8 %fusion = (bf16[1,88,1024]{2,1,0:T(8,128)(2,1)}, bf16[1,88,1024]{2,1,0:T(8,128)(2,1)}) fusion(bf16[2,88,1024]{2,1,0:T(8,128)(2,1)} %bitcast.25), kind=kLoop, calls=%fused_computation | loop fusion | bytes 720896 | tf_op jit(solution)/shard_map/slice | solution.py:220
  8.3 0.0 copy-start.4
  8.3 0.0 copy-start.10
  8.3 0.0 copy-start.12
  8.3 0.0 copy-start.13
  8.3 0.0 all-gather.7.cloned.1.call-update
  8.3 0.0 all-gather.5.cloned.1.call-start
  8.4 0.7 all-gather.5.cloned.1.call-update
  9.1 0.0 copy-start.3
  9.1 0.9 copy-done.3
  10.1 0.0 copy-start.5
  10.1 0.9 copy-done.5
  11.0 0.0 copy-start.6
  11.0 0.9 copy-done.6
  12.0 0.0 copy-start.7
  12.0 0.9 copy-done.7
  12.9 0.0 copy-start.8
  12.9 0.9 copy-done.8
  13.9 0.0 copy-start.9
  13.9 0.9 copy-done.9
  14.8 0.0 copy-start.11
  14.8 0.7 copy-done.11
  15.5 0.0 copy-start.14
  15.5 0.7 copy-done.14
  16.1 0.0 copy-start.15
  16.2 0.7 copy-done.15
  16.8 0.0 copy-start
  16.8 2.4 %attention.1 = bf16[128,1024]{1,0:T(8,128)(2,1)} custom-call(bf16[128,1024]{1,0:T(8,128)(2,1)S(1)} %copy-done.3, f32[1,1024]{1,0:T(1,128)S(1)} %bitcast.19, bf16[1024,128]{1,0:T(8,128)(2,1)S(1)} %copy-done.5, bf16[1024,128]{1,0:T(8,128)(2,1)S(1)} %copy-done.6, bf16[1024,128]{1,0:T(8,128)(2,1)S(1)} %copy-done.7, bf16[128,1024]{1,0:T(8,128)(2,1)S(1)} %copy-done.8, ...), custom_call_target="tpu_custom_call" | custom-call | tf_op jit(solution)/shard_map/attention/pallas_call | solution.py:222
  19.2 9.2 %all-to-all-start = ((bf16[8,16,1024]{2,1,0:T(8,128)(2,1)}), bf16[8,16,1024]{2,1,0:T(8,128)(2,1)S(1)}, u32[]{:S(2)}, u32[]{:S(2)}) async-start(bf16[8,16,1024]{2,1,0:T(8,128)(2,1)} %bitcast.3), calls=%async_computation | async-start | bytes 524288 | tf_op jit(solution)/shard_map/all_to_all | solution.py:241
  28.4 5.6 %all-to-all-done.parts_ref = bf16[8,16,1024]{2,1,0:T(8,128)(2,1)S(1)} async-done(((bf16[8,16,1024]{2,1,0:T(8,128)(2,1)}), bf16[8,16,1024]{2,1,0:T(8,128)(2,1)S(1)}, u32[]{:S(2)}, u32[]{:S(2)}) %all-to-all-start) | async-done | bytes 262176 | tf_op jit(solution)/shard_map/all_to_all | solution.py:241
  34.0 0.0 copy-done.4
  34.0 0.0 copy-done.10
  34.0 0.0 copy-done.12
  34.0 0.0 copy-done.13
  34.0 0.7 dispatch.1
  34.7 23.7 %all_to_all.20 = bf16[16,24,128]{2,1,0:T(8,128)(2,1)S(1)} all-to-all(bf16[16,24,128]{2,1,0:T(8,128)(2,1)S(1)} %bitcast.17), channel_id=1, replica_groups=mesh['z'=16,'y'=4,'x'=4,'c'=2] {'z'}, dimensions={0} | all-to-all | bytes 196608 | tf_op jit(solution)/shard_map/all_to_all | solution.py:255
  58.3 13.4 %all_gather.9.tokens_ref = bf16[4,384,128]{2,1,0:T(8,128)(2,1)S(1)} all-gather(bf16[1,384,128]{2,1,0:T(8,128)(2,1)S(1)} %bitcast.24), channel_id=1, replica_groups=mesh['z'=16,'y'=4,'x'=4,'c'=2] {'y'}, dimensions={0}, use_global_device_ids=true | all-gather | bytes 491520 | tf_op jit(solution)/shard_map/all_gather | solution.py:256
  71.8 0.0 all-gather.7.cloned.1.call-done
  71.8 6.7 %all-gather.5.cloned.1.call-done = bf16[1,704,1024]{2,1,0:T(8,128)(2,1)} async-done(((bf16[1,88,1024]{2,1,0:T(8,128)(2,1)}), bf16[1,704,1024]{2,1,0:T(8,128)(2,1)}) %all-gather.5.cloned.1.call-update) | async-done | bytes 1441808 | tf_op jit(solution)/shard_map/all_gather | solution.py:219
  78.5 0.0 copy-done
  78.5 0.0 copy-start.1
  78.5 1.4 %copy-done.1 = bf16[1,704,1024]{2,1,0:T(8,128)(2,1)S(1)} copy-done((bf16[1,704,1024]{2,1,0:T(8,128)(2,1)S(1)}, bf16[1,704,1024]{2,1,0:T(8,128)(2,1)}, u32[]{:S(2)}) %copy-start.1) | copy-done | bytes 1441816
  79.9 0.0 copy-start.2
  79.9 1.4 %copy-done.2 = bf16[1,704,1024]{2,1,0:T(8,128)(2,1)S(1)} copy-done((bf16[1,704,1024]{2,1,0:T(8,128)(2,1)S(1)}, bf16[1,704,1024]{2,1,0:T(8,128)(2,1)}, u32[]{:S(2)}) %copy-start.2) | copy-done | bytes 1441816
  81.2 2.3 %ffn.1 = bf16[4,384,128]{2,1,0:T(8,128)(2,1)S(1)} custom-call(bf16[4,384,128]{2,1,0:T(8,128)(2,1)S(1)} %all_gather.9.tokens_ref, bf16[704,1024]{1,0:T(8,128)(2,1)S(1)} %bitcast.15, bf16[704,1024]{1,0:T(8,128)(2,1)S(1)} %bitcast.14, bf16[704,1024]{1,0:T(8,128)(2,1)S(1)} %copy-done), custom_call_target="tpu_custom_call" | custom-call | tf_op jit(solution)/shard_map/ffn/pallas_call | solution.py:257
  83.5 12.5 %all_to_all.21 = bf16[4,384,128]{2,1,0:T(8,128)(2,1)S(1)} all-to-all(bf16[4,384,128]{2,1,0:T(8,128)(2,1)S(1)} %ffn.1), channel_id=1, replica_groups=mesh['z'=16,'y'=4,'x'=4,'c'=2] {'y'}, dimensions={0} | all-to-all | bytes 786432 | tf_op jit(solution)/shard_map/all_to_all | solution.py:266
  96.1 0.1 reduce_sum.12
  96.1 25.3 %all_to_all.22 = bf16[16,24,128]{2,1,0:T(8,128)(2,1)S(1)} all-to-all(bf16[16,24,128]{2,1,0:T(8,128)(2,1)S(1)} %bitcast.23), channel_id=1, replica_groups=mesh['z'=16,'y'=4,'x'=4,'c'=2] {'z'}, dimensions={0} | all-to-all | bytes 196608 | tf_op jit(solution)/shard_map/all_to_all | solution.py:268
  121.4 1.1 combine.1
Async XLA Ops:
  6.5 65.2 %all-gather.7.cloned.1.call-start = ((), (), s32[]{:S(2)}) async-start(), calls=%async_computation.5 | async-start | bytes 1622016 | tf_op jit(solution)/shard_map/all_gather | solution.py:220
  8.3 25.7 %copy-start.4 = (bf16[128,1024]{1,0:T(8,128)(2,1)S(1)}, bf16[128,1024]{1,0:T(8,128)(2,1)}, u32[]{:S(2)}) copy-start(bf16[128,1024]{1,0:T(8,128)(2,1)} %resid_ref.3) | copy-start | bytes 786436
  8.3 25.7 %copy-start.10 = (bf16[1024,16]{0,1:T(8,128)(2,1)S(1)}, bf16[1024,16]{0,1:T(8,128)(2,1)}, u32[]{:S(2)}) copy-start(bf16[1024,16]{0,1:T(8,128)(2,1)} %param.24) | copy-start | bytes 98308
  8.3 25.7 %copy-start.12 = (f32[1024]{0:T(1024)S(1)}, f32[1024]{0:T(1024)}, u32[]{:S(2)}) copy-start(f32[1024]{0:T(1024)} %param.23) | copy-start | bytes 12292
  8.3 25.7 %copy-start.13 = (s32[128,2]{0,1:T(2,128)S(1)}, s32[128,2]{0,1:T(2,128)}, u32[]{:S(2)}) copy-start(s32[128,2]{0,1:T(2,128)} %param.25) | copy-start | bytes 3076
  8.3 70.2 %all-gather.5.cloned.1.call-start = ((), (), s32[]{:S(2)}) async-start(), calls=%async_computation.4 | async-start | bytes 1622016 | tf_op jit(solution)/shard_map/all_gather | solution.py:219
  9.1 1.0 copy-start.3
  10.1 0.9 copy-start.5
  11.0 0.9 copy-start.6
  12.0 0.9 copy-start.7
  12.9 0.9 copy-start.8
  13.9 0.9 copy-start.9
  14.8 0.7 copy-start.11
  15.5 0.7 copy-start.14
  16.1 0.7 copy-start.15
  16.8 61.7 %copy-start = (bf16[704,1024]{1,0:T(8,128)(2,1)S(1)}, bf16[704,1024]{1,0:T(8,128)(2,1)}, u32[]{:S(2)}) copy-start(bf16[704,1024]{1,0:T(8,128)(2,1)} %down_ref.1) | copy-start | bytes 4325380
  19.2 14.8 %all-to-all-start = ((bf16[8,16,1024]{2,1,0:T(8,128)(2,1)}), bf16[8,16,1024]{2,1,0:T(8,128)(2,1)S(1)}, u32[]{:S(2)}, u32[]{:S(2)}) async-start(bf16[8,16,1024]{2,1,0:T(8,128)(2,1)} %bitcast.3), calls=%async_computation | async-start | bytes 524288 | tf_op jit(solution)/shard_map/all_to_all | solution.py:241
  78.5 1.4 %copy-start.1 = (bf16[1,704,1024]{2,1,0:T(8,128)(2,1)S(1)}, bf16[1,704,1024]{2,1,0:T(8,128)(2,1)}, u32[]{:S(2)}) copy-start(bf16[1,704,1024]{2,1,0:T(8,128)(2,1)} %all-gather.7.cloned.1.call-done) | copy-start | bytes 4325380
  79.9 1.4 %copy-start.2 = (bf16[1,704,1024]{2,1,0:T(8,128)(2,1)S(1)}, bf16[1,704,1024]{2,1,0:T(8,128)(2,1)}, u32[]{:S(2)}) copy-start(bf16[1,704,1024]{2,1,0:T(8,128)(2,1)} %all-gather.5.cloned.1.call-done) | copy-start | bytes 4325380
Sparse Core Ops, SparseCore 0:
  9.5 35.0 all-gather.6
  46.7 31.7 all-gather.4
